TPU v7x, 256 devices: a whole 4x4x8 slice. The times are simulated.
256 devices in a mesh: patch: 128 (over z, y, x), slab: 2 (over core).
Axes of the slice: x: 4, y: 4, z: 8, core: 2. Of those that a mesh axis runs over, the one named last changes fastest.
Arguments:
- field: float32 [128, 128, 3, 64, 128], P('patch', 'slab'), may hold values from -6 to 6
- xmats: float32 [128, 2, 64, 64], P('patch'), may hold values from -0.75 to 0.75
- ymats: float32 [128, 2, 128, 128], P('patch'), may hold values from -0.5 to 0.5
- zmats: float32 [128, 2, 128, 128], P('patch'), may hold values from -0.5 to 0.5
- coupling: float32 [128, 3, 3], P('patch'), may hold values from -3.5 to 3.5
- mortar_z: float32 [128, 4, 32, 128], P('patch'), may hold values from -0.5 to 0.5
- mortar_x: float32 [128, 2, 64, 128], P('patch'), may hold values from -0.5 to 0.5
- mortar_y: float32 [128, 2, 64, 64], P('patch'), may hold values from -0.75 to 0.75
- matching: int32 [128, 4], P('patch'), may hold values from 0 to 511, as said below
- orient: int32 [128, 4], P('patch'), may hold values from 0 to 3, as said below
- sizes: int32 [128, 2], P('patch'), may hold values from 32 to 128, as said below
Outputs:
- applied: float32 [128, 128, 3, 64, 128], P('patch', 'slab')
Inputs may be any that keep to these rules, and one draw needn't show every extreme that they name: matching[p, f] = 4 q + g says that face f of patch p is glued to face g of patch q; the gluing is symmetric and never joins a face to itself. `orient`: both faces of a gluing carry the same code. sizes[p, 0] lies in 32 to 64, sizes[p, 1] in 64 to 128; some patch has all cells active.
All inputs are finite; a program needn't handle non-finite values.
Results may differ from a plain program's by a relative error of at most 0.0003.
Values sent between devices are 32-bit elements; how exact they have to be, the bound alone decides.
A program may use at most 192 MiB of HBM per device.

v0:
```python
import functools

import jax
import jax.numpy as jnp
from jax import lax
from jax.experimental import pallas as pl
from jax.experimental.pallas import tpu as pltpu
from jax.sharding import PartitionSpec as P

MESH = pl.DeviceIdType.MESH
F32 = jnp.float32
BF16 = jnp.bfloat16
MAT = (((1,), (0,)), ((), ()))
NT = (((1,), (1,)), ((), ()))


def split(a):
    hi = a.astype(BF16)
    return hi, (a - hi.astype(F32)).astype(BF16)


def bdot(a, b, dims=MAT):
    return lax.dot_general(a, b, dims, preferred_element_type=F32)


def dot3(a, b, dims=MAT):
    ah, al = split(a)
    bh, bl = split(b)
    return bdot(ah, bh, dims) + (bdot(ah, bl, dims) + bdot(al, bh, dims))


def rows(ref, start, count, stride):
    return ref[pl.ds(start, count, stride=stride), :]


def face_rows(sizes_ref, mx_ref, my_ref, e_ref):
    e_ref[...] = jnp.zeros((256, 384), F32)
    lane = lax.broadcasted_iota(jnp.int32, (32, 128), 1)
    lane64 = lax.broadcasted_iota(jnp.int32, (32, 64), 1)
    zero = jnp.zeros((32, 64), F32)
    for h in range(2):
        for f in range(2):
            at = h * 128 + f * 32
            j = h * 32
            e_ref[at : at + 32, f * 128 : f * 128 + 128] = jnp.where(
                lane < sizes_ref[0, 1], mx_ref[f, j : j + 32], 0.0
            )
            e = jnp.where(lane64 < sizes_ref[0, 0], my_ref[f, j : j + 32], 0.0)
            e_ref[at + 64 : at + 96, 256:384] = jnp.concatenate(
                [e, zero] if f == 0 else [zero, e], axis=1
            )


def trace_part(sizes_ref, block, t_ref):
    flat = block.reshape(64 * 192, 128)
    sx, sy = sizes_ref[0, 0], sizes_ref[0, 1]
    lane = lax.broadcasted_iota(jnp.int32, (64, 128), 1)
    for d in range(3):

        def body(x, accs):
            low, high = accs
            v = pltpu.roll(rows(flat, d * 64 + x, 64, 192), x, 1)
            low = jnp.where(lane == x, v, low)
            high = jnp.where(lane == lax.rem(x + sy - 1, 128), v, high)
            return low, high

        zero = jnp.zeros((64, 128), F32)
        low, high = lax.fori_loop(0, 64, body, (zero, zero), unroll=8)
        high = pltpu.roll(high, lax.rem(193 - sy, 128), 1)
        at = d * 64
        t_ref[at : at + 64, 0:128] = rows(flat, d * 64, 64, 192)
        t_ref[at : at + 64, 128:256] = rows(flat, d * 64 + jnp.maximum(sx - 1, 0), 64, 192)
        t_ref[at : at + 64, 256:384] = jnp.where(lane < 64, low, high)


def mortar_part(t_ref, s, mz_ref, e_ref):
    along = dot3(t_ref[...], e_ref[...], NT)
    mz = pltpu.roll(mz_ref[...].reshape(128, 128), lax.rem(128 - s * 64, 128), 1)[:, :64]
    face = lax.broadcasted_iota(jnp.int32, (32, 256), 1) % 128 // 32
    parts = []
    for d in range(3):
        full = dot3(mz, along[d * 64 : d * 64 + 64])
        out = jnp.where(face == 0, full[:32], full[32:64])
        out = jnp.where(face == 2, full[64:96], out)
        parts.append(jnp.where(face == 3, full[96:], out))
    return parts


def zy_weights(sizes_ref, s, zm_ref, ym_ref, zl, yw):
    z_rows = [zm_ref[m, pl.ds(pl.multiple_of(s * 64, 64), 64), :] for m in range(2)]
    az = pltpu.roll(jnp.concatenate(z_rows, axis=0), lax.rem(128 - s * 64, 128), 1)
    hi, lo = split(az)
    zl[:128, :128] = hi
    zl[:128, 128:] = hi
    zl[128:, :128] = lo
    zl[128:, 128:] = jnp.zeros_like(lo)
    zero = jnp.zeros((128, 128), BF16)
    sy = sizes_ref[0, 1]
    active = (lax.broadcasted_iota(jnp.int32, (128, 128), 0) < sy) & (
        lax.broadcasted_iota(jnp.int32, (128, 128), 1) < sy
    )
    for k, m in ((0, 1), (256, 0), (512, 1)):
        hi, lo = split(jnp.transpose(jnp.where(active, ym_ref[m], 0.0)))
        yw[k : k + 128, :128] = hi
        yw[k : k + 128, 128:] = lo
        yw[k + 128 : k + 256, :128] = hi
        yw[k + 128 : k + 256, 128:] = zero


def zy_chunk(k, own2, other2, zl, yw, tb, out):
    for pair in range(12):
        tops, lows = [], []
        for n in (2 * pair, 2 * pair + 1):
            start = n // 8 * 64 + n % 8 + k * 8
            top, low = split(
                jnp.concatenate([rows(own2, start, 64, 192), rows(other2, start, 64, 192)], axis=0)
            )
            tops.append(top)
            lows.append(low)
        w = jnp.concatenate(
            [jnp.concatenate(tops, axis=1), jnp.concatenate(lows, axis=1)], axis=0
        )
        r = bdot(zl[...], w)
        t = r[:128] + r[128:]
        for n in range(2):
            at = (2 * pair + n) * 64
            sh, sl = split(t[:64, n * 128 : n * 128 + 128])
            mh, ml = split(t[64:, n * 128 : n * 128 + 128])
            tb[at : at + 64, 0:128] = mh
            tb[at : at + 64, 128:256] = ml
            tb[at : at + 64, 256:384] = sh
            tb[at : at + 64, 384:512] = sl
    for d in range(3):
        at = d * 512
        a = bdot(tb[at : at + 512, :256], yw[:256])
        out[0, d] = (a[:, :128] + a[:, 128:]).reshape(8, 64, 128)
        b = bdot(tb[at : at + 512, :], yw[256:])
        out[1, d] = (b[:, :128] + b[:, 128:]).reshape(8, 64, 128)


def front_kernel(
    sizes_ref, match_ref, field, zm, ym, mz, mx, my, own_ref, near_ref, mid,
    block, other, zm_ref, ym_ref, mz_ref, mx_ref, my_ref, e_ref, t_ref, zl, yw, tb, stage,
    part, got, mine, gath, sendb, mt, mts,
    lsem, wsem, osem, fsem, psem, asem, bsem, csem, dsem,
):
    p = lax.axis_index("patch")
    s = lax.axis_index("slab")
    z, y, x = p // 16, p // 4 % 4, p % 4
    me = z * 4 + x

    def dev(a, yy):
        return (a // 4 * 16 + yy * 4 + a % 4, s)

    partner = (p, 1 - s)

    def copy(src, dst, sem, k, where):
        return pltpu.make_async_remote_copy(
            src, dst, sem.at[0, k], sem.at[1, k], device_id=where, device_id_type=MESH
        )

    barrier = pltpu.get_barrier_semaphore()

    def greet(d, c):
        pl.semaphore_signal(
            barrier, inc=1, device_id=dev((me + d) % 32, y), device_id_type=MESH
        )
        return c

    pl.semaphore_signal(barrier, inc=1, device_id=partner, device_id_type=MESH)
    lax.fori_loop(1, 32, greet, 0)

    def greet_y(d, c):
        pl.semaphore_signal(
            barrier, inc=1, device_id=dev(me, (y + d) % 4), device_id_type=MESH
        )
        return c

    lax.fori_loop(1, 4, greet_y, 0)

    load = pltpu.make_async_copy(field.at[0], block, lsem.at[0])
    load.start()
    smalls = [
        pltpu.make_async_copy(a.at[0], b, wsem.at[n])
        for n, (a, b) in enumerate(
            ((zm, zm_ref), (ym, ym_ref), (mz, mz_ref), (mx, mx_ref), (my, my_ref))
        )
    ]
    for c in smalls:
        c.start()
    for c in smalls:
        c.wait()
    face_rows(sizes_ref, mx_ref, my_ref, e_ref)
    zy_weights(sizes_ref, s, zm_ref, ym_ref, zl, yw)
    lane1 = lax.broadcasted_iota(jnp.int32, (1, 128), 1)
    row = jnp.where(lane1 == 0, match_ref[0, 0], match_ref[0, 1])
    row = jnp.where(lane1 == 2, match_ref[0, 2], row)
    mt[me] = jnp.where(lane1 == 3, match_ref[0, 3], row)
    load.wait()
    trace_part(sizes_ref, block, t_ref)
    pl.semaphore_wait(barrier, 35)

    def field_copy(k):
        at = pl.ds(pl.multiple_of(k * 8, 8), 8)
        return copy(field.at[0, :, :, at], other.at[:, :, at], fsem, k, partner)

    def start_field(k, c):
        field_copy(k).start()
        return c

    lax.fori_loop(0, 8, start_field, 0)

    def match_copy(d):
        return copy(mt.at[me], mt.at[me], asem, d, dev((me + d) % 32, y))

    def start_match(d, c):
        match_copy(d).start()
        return c

    lax.fori_loop(1, 32, start_match, 0)

    parts = mortar_part(t_ref, s, mz_ref, e_ref)
    half = s == 0
    for d in range(3):
        part[d] = jnp.where(half, parts[d][:, 128:], parts[d][:, :128])
    c0 = copy(part, got, psem, 0, partner)
    c0.start()
    for d in range(3):
        mine[:, d, :] = jnp.where(half, parts[d][:, :128], parts[d][:, 128:])
    mine[:, 3, :] = jnp.zeros((32, 128), F32)

    own2 = block.reshape(64 * 192, 128)
    other2 = other.reshape(64 * 192, 128)

    def mid_copy(k):
        at = pl.ds(pl.multiple_of(k * 8, 8), 8)
        return pltpu.make_async_copy(stage.at[k % 2], mid.at[:, :, at], osem.at[k % 2])

    def chunks(lo, hi):
        def one(k, c):
            field_copy(k).wait()

            @pl.when(k >= 2)
            def _():
                mid_copy(k - 2).wait()

            zy_chunk(k, own2, other2, zl, yw, tb, stage.at[k % 2])
            mid_copy(k).start()
            return c

        lax.fori_loop(lo, hi, one, 0)

    chunks(0, CUTS[0])
    c0.wait()
    for d in range(3):
        mine[:, d, :] = mine[:, d, :] + got[d]

    def spread_copy(d):
        a = (me + d) % 32
        return copy(mine.at[a], gath.at[y, me], bsem, d, dev(a, y))

    def start_spread(d, c):
        spread_copy(d).start()
        return c

    lax.fori_loop(1, 32, start_spread, 0)
    cm = copy(mine, own_ref.at[s], psem, 1, partner)
    cm.start()
    own_ref[s] = mine[...]
    gath[y, me] = mine[me]

    def wait_match(d, c):
        match_copy(d).wait()
        return c

    lax.fori_loop(1, 32, wait_match, 0)
    tos = pltpu.make_async_copy(mt, mts, lsem.at[1])
    tos.start()
    chunks(CUTS[0], CUTS[1])

    def wait_spread(d, c):
        spread_copy(d).wait()
        return c

    lax.fori_loop(1, 32, wait_spread, 0)

    def line_copy(d):
        return copy(gath.at[y], gath.at[y], csem, d, dev(me, (y + d) % 4))

    for d in range(1, 4):
        line_copy(d).start()
    tos.wait()
    chunks(CUTS[1], CUTS[2])
    for d in range(1, 4):
        line_copy(d).wait()

    lane4 = lax.broadcasted_iota(jnp.int32, (4, 128), 1) // 32

    def pick(a, c):
        out = jnp.zeros((4, 128), F32)
        for f in range(4):
            m = mts[a, 0, f]
            q = m // 4
            v = gath[q // 4 % 4, q // 16 * 4 + q % 4]
            v = pltpu.roll(v, (f + 4 - m % 4) % 4 * 32, 1)
            out = jnp.where(lane4 == f, v, out)
        sendb[a] = out
        return c

    lax.fori_loop(0, 32, pick, 0, unroll=4)

    def back_copy(d):
        a = (me + d) % 32
        return copy(sendb.at[a], near_ref.at[s, me], dsem, d, dev(a, y))

    def start_back(d, c):
        back_copy(d).start()
        return c

    lax.fori_loop(1, 32, start_back, 0)
    near_ref[s, me] = sendb[me]
    chunks(CUTS[2], 8)

    def wait_back(d, c):
        back_copy(d).wait()
        return c

    lax.fori_loop(1, 32, wait_back, 0)
    cn = copy(near_ref.at[s], near_ref.at[s], psem, 2, partner)
    cn.start()
    cm.wait()
    mid_copy(6).wait()
    mid_copy(7).wait()
    cn.wait()


CUTS = (1, 4, 6)


def front(sizes, matching, field, zm, ym, mz, mx, my):
    vmem = pl.BlockSpec(memory_space=pltpu.VMEM)
    smem = pl.BlockSpec(memory_space=pltpu.SMEM)
    hbm = pl.BlockSpec(memory_space=pl.ANY)
    dma = pltpu.SemaphoreType.DMA
    shape = jax.ShapeDtypeStruct((2, 32, 4, 128), F32)
    return pl.pallas_call(
        front_kernel,
        out_shape=(shape, shape, jax.ShapeDtypeStruct((2, 3, 64, 64, 128), F32)),
        in_specs=[smem, smem] + [hbm] * 6,
        out_specs=(vmem, vmem, hbm),
        scratch_shapes=[
            pltpu.VMEM((64, 3, 64, 128), F32),
            pltpu.VMEM((64, 3, 64, 128), F32),
            pltpu.VMEM((2, 128, 128), F32),
            pltpu.VMEM((2, 128, 128), F32),
            pltpu.VMEM((4, 32, 128), F32),
            pltpu.VMEM((2, 64, 128), F32),
            pltpu.VMEM((2, 64, 64), F32),
            pltpu.VMEM((256, 384), F32),
            pltpu.VMEM((192, 384), F32),
            pltpu.VMEM((256, 256), BF16),
            pltpu.VMEM((768, 256), BF16),
            pltpu.VMEM((1536, 512), BF16),
            pltpu.VMEM((2, 2, 3, 8, 64, 128), F32),
            pltpu.VMEM((3, 32, 128), F32),
            pltpu.VMEM((3, 32, 128), F32),
            pltpu.VMEM((32, 4, 128), F32),
            pltpu.VMEM((4, 32, 4, 128), F32),
            pltpu.VMEM((32, 4, 128), F32),
            pltpu.VMEM((32, 1, 128), jnp.int32),
            pltpu.SMEM((32, 1, 128), jnp.int32),
            dma((2,)), dma((5,)), dma((2,)), dma((2, 8)), dma((2, 3)),
            dma((2, 32)), dma((2, 32)), dma((2, 4)), dma((2, 32)),
        ],
        compiler_params=pltpu.CompilerParams(
            collective_id=0, has_side_effects=True, vmem_limit_bytes=60 * 2**20
        ),
        name="front",
    )(sizes, matching, field, zm, ym, mz, mx, my)


def turned(size, low, mask, flags):
    r = lax.broadcasted_iota(jnp.int32, (size, size), 0)
    c = lax.broadcasted_iota(jnp.int32, (size, size), 1)
    face = r // 32 % 4
    flag = jnp.where(face == 0, flags[0], flags[1])
    flag = jnp.where(face == 2, flags[2], flag)
    flag = jnp.where(face == 3, flags[3], flag)
    return jnp.where(c == (r ^ jnp.where(flag == 1, mask, 0)), 1.0, 0.0).astype(BF16)


def back_part(orient_ref, own_ref, near_ref, mz_ref, e_ref, s, bx, by):
    codes = [orient_ref[0, f] for f in range(4)]
    face = lax.broadcasted_iota(jnp.int32, (32, 128), 1) // 32
    own2 = own_ref.reshape(256, 128)
    near2 = near_ref.reshape(256, 128)
    mz = pltpu.roll(mz_ref[...].reshape(128, 128), lax.rem(128 - s * 64, 128), 1)
    zh, zlo = split(jnp.transpose(mz)[:64])
    perm = turned(128, 5, 31, [c % 2 for c in codes])
    mats = (
        (own2, zh, zlo),
        (near2, bdot(zh, perm).astype(BF16), bdot(zlo, perm).astype(BF16)),
    )
    cols = []
    for data, mh, ml in mats:
        for h in range(2):
            per = []
            for c in range(3):
                v = rows(data, h * 128 + c, 32, 4)
                wide = jnp.concatenate(
                    [jnp.where(face == f, v, 0.0) for f in range(4)], axis=0
                )
                wh, wl = split(wide)
                per.append(bdot(mh, wh) + (bdot(ml, wh) + bdot(mh, wl)))
            cols.append(jnp.concatenate(per, axis=0))
    ch, cl = split(jnp.concatenate(cols, axis=1))
    eh, el = split(e_ref[...])
    perm = turned(256, 5, 159, [c // 2 for c in codes])
    eh = jnp.concatenate([eh, (-bdot(perm, eh)).astype(BF16)], axis=0)
    el = jnp.concatenate([el, (-bdot(perm, el)).astype(BF16)], axis=0)
    back = bdot(ch, eh) + (bdot(ch, el) + bdot(cl, eh))
    for c in range(3):
        r = back[c * 64 : c * 64 + 64]
        bx[0, c] = r[:, :128]
        bx[1, c] = r[:, 128:256]
        col = r[:, 256:]
        by[c] = jnp.transpose(jnp.concatenate([col, col], axis=0))


def last_kernel(
    sizes_ref, cpl, orient_ref, data, xm_ref, own_ref, near_ref, mz_ref, mx_ref, my_ref, out,
    xl, e_ref, bx, by,
):
    i = pl.program_id(0)
    sx, sy = sizes_ref[0, 0], sizes_ref[0, 1]

    @pl.when(i == 0)
    def _():
        active = (lax.broadcasted_iota(jnp.int32, (64, 64), 0) < sx) & (
            lax.broadcasted_iota(jnp.int32, (64, 64), 1) < sx
        )
        h0, l0 = split(jnp.where(active, xm_ref[0], 0.0))
        h1, l1 = split(jnp.where(active, xm_ref[1], 0.0))
        hi = jnp.concatenate([h0, h1], axis=1)
        xl[:64, :128] = hi
        xl[:64, 128:] = hi
        xl[64:, :128] = jnp.concatenate([l0, l1], axis=1)
        xl[64:, 128:] = jnp.zeros((64, 128), BF16)
        face_rows(sizes_ref, mx_ref, my_ref, e_ref)
        back_part(orient_ref, own_ref, near_ref, mz_ref, e_ref, lax.axis_index("slab"), bx, by)

    row = lax.broadcasted_iota(jnp.int32, (64, 128), 0)
    lane = lax.broadcasted_iota(jnp.int32, (64, 128), 1)
    first_x = row == 0
    last_x = row == sx - 1
    first_y = lane == 0
    last_y = lane == sy - 1
    flat = data.reshape(2 * 3 * 64 * 8, 128)
    cols = [pltpu.roll(by[c], lax.rem(128 - i * 8, 128), 1) for c in range(3)]
    for pair in range(4):
        inner = []
        for d in range(3):
            tops, lows = [], []
            for n in range(2):
                k = pair * 2 + n
                first = rows(flat, d * 512 + k, 64, 8)
                second = rows(flat, 1536 + d * 512 + k, 64, 8)
                top, low = split(jnp.concatenate([first, second], axis=0))
                tops.append(top)
                lows.append(low)
            w = jnp.concatenate(
                [jnp.concatenate(tops, axis=1), jnp.concatenate(lows, axis=1)], axis=0
            )
            r = bdot(xl[...], w)
            inner.append(r[:64] + r[64:])
        for c in range(3):
            mix = cpl[0, c, 0] * inner[0] + cpl[0, c, 1] * inner[1] + cpl[0, c, 2] * inner[2]
            for n in range(2):
                k = pair * 2 + n
                v = mix[:, n * 128 : n * 128 + 128]
                zrow = pl.ds(i * 8 + k, 1)
                v = v + jnp.where(first_x, bx[0, c, zrow, :], 0.0)
                v = v + jnp.where(last_x, bx[1, c, zrow, :], 0.0)
                v = v + jnp.where(first_y, cols[c][:64, k : k + 1], 0.0)
                v = v + jnp.where(last_y, cols[c][64:, k : k + 1], 0.0)
                out[k, c] = v


def first_spread(sizes, cpl, orient, data, xm, own, near, mz, mx, my):
    smem = pl.BlockSpec(memory_space=pltpu.SMEM)
    whole = lambda *shape: pl.BlockSpec(shape, lambda i: (0,) * len(shape))
    return pl.pallas_call(
        last_kernel,
        grid=(8,),
        out_shape=jax.ShapeDtypeStruct((1, 64, 3, 64, 128), F32),
        in_specs=[
            smem,
            smem,
            smem,
            pl.BlockSpec((2, 3, 64, 8, 128), lambda i: (0, 0, 0, i, 0)),
            whole(None, 2, 64, 64),
            whole(2, 32, 4, 128),
            whole(2, 32, 4, 128),
            whole(None, 4, 32, 128),
            whole(None, 2, 64, 128),
            whole(None, 2, 64, 64),
        ],
        out_specs=pl.BlockSpec((None, 8, 3, 64, 128), lambda i: (0, i, 0, 0, 0)),
        scratch_shapes=[
            pltpu.VMEM((128, 256), BF16),
            pltpu.VMEM((256, 384), F32),
            pltpu.VMEM((2, 3, 64, 128), F32),
            pltpu.VMEM((3, 128, 128), F32),
        ],
        compiler_params=pltpu.CompilerParams(vmem_limit_bytes=60 * 2**20),
        name="first_spread",
    )(sizes, cpl, orient, data, xm, own, near, mz, mx, my)


def per_device(
    field, xmats, ymats, zmats, coupling, mortar_z, mortar_x, mortar_y, matching, orient, sizes
):
    own, near, mid = front(sizes, matching, field, zmats, ymats, mortar_z, mortar_x, mortar_y)
    return first_spread(
        sizes, coupling, orient, mid, xmats, own, near, mortar_z, mortar_x, mortar_y
    )


def solution(mesh):
    in_specs = (
        P("patch", "slab", None, None, None),
        P("patch", None, None, None),
        P("patch", None, None, None),
        P("patch", None, None, None),
        P("patch", None, None),
        P("patch", None, None, None),
        P("patch", None, None, None),
        P("patch", None, None, None),
        P("patch", None),
        P("patch", None),
        P("patch", None),
    )
    return jax.shard_map(
        per_device,
        mesh=mesh,
        in_specs=in_specs,
        out_specs=P("patch", "slab", None, None, None),
        check_vma=False,
    )
```

profile of v0, /device:TPU:1, one launch (start us, length us, event | category | flops | bytes accessed | tf_op | source)
XLA Modules:
  0.0 69.3 jit_solution(8232302938680707485)
XLA Ops:
  0.0 1.3 %copy.12.cpl = f32[1,3,3]{2,1,0:T(4,128)} copy(f32[1,3,3]{2,0,1:T(1,128)} %param.15) | data formatting | bytes 72 | tf_op args[4]
  1.3 54.6 %front.1 = (f32[2,32,4,128]{3,2,1,0:T(4,128)}, f32[2,32,4,128]{3,2,1,0:T(4,128)}, f32[2,3,64,64,128]{4,3,2,1,0:T(8,128)}) custom-call(s32[1,2]{1,0:T(1,128)} %sizes_ref.3, s32[1,4]{1,0:T(1,128)} %match_ref.1, f32[1,64,3,64,128]{4,3,2,1,0:T(8,128)} %field.1, f32[1,2,128,128]{3,2,1,0:T(8,128)} %zm.1, f32[1,2,128,128]{3,2,1,0:T(8,128)} %ym.1, ...), custom_call_target="tpu_custom_call" | custom-call | tf_op jit(solution)/shard_map/front/pallas_call | solution.py:346
  55.9 13.4 %first_spread.1 = f32[1,64,3,64,128]{4,3,2,1,0:T(8,128)} custom-call(s32[1,2]{1,0:T(1,128)} %sizes_ref.3, f32[1,3,3]{2,1,0:T(4,128)} %copy.12.cpl, s32[1,4]{1,0:T(1,128)} %orient_ref.1, f32[2,3,64,64,128]{4,3,2,1,0:T(8,128)} %get-tuple-element.8.data, f32[1,2,64,64]{3,2,1,0:T(8,128)} %xm_ref.1, f32[2,32,4,128]{3,2,1,0:T(4,128)} %get-tuple-element.9.own_ref, ...), custom_call_target="tpu_custom_call" | custom-call | tf_op jit(solution)/shard_map/first_spread/pallas_call | solution.py:492
where the time goes:
time: 69.5 us; the launch traced here: 69.3 us
  Pallas kernels  68 us (98%)
  local copies, waits for them, and re-layouts  1.27 us (2%)
    pallas_call x1, Pallas kernels, front(): pl.pallas_call(front_kernel, out_shape=(shape, shape, jax.ShapeDtypeStruc...  54.6 us
    pallas_call x1, Pallas kernels, first_spread(): pl.pallas_call(last_kernel, grid=(8,), out_shape=jax.ShapeDtypeStruct((1,...  13.4 us

commit v1 on v0

--- a/solution.py
+++ b/solution.py
@@ -52,14 +52,13 @@
 
 
 def trace_part(sizes_ref, block, t_ref):
-    flat = block.reshape(64 * 192, 128)
     sx, sy = sizes_ref[0, 0], sizes_ref[0, 1]
     lane = lax.broadcasted_iota(jnp.int32, (64, 128), 1)
     for d in range(3):
 
         def body(x, accs):
             low, high = accs
-            v = pltpu.roll(rows(flat, d * 64 + x, 64, 192), x, 1)
+            v = pltpu.roll(block[d, x], x, 1)
             low = jnp.where(lane == x, v, low)
             high = jnp.where(lane == lax.rem(x + sy - 1, 128), v, high)
             return low, high
@@ -68,8 +67,8 @@
         low, high = lax.fori_loop(0, 64, body, (zero, zero), unroll=8)
         high = pltpu.roll(high, lax.rem(193 - sy, 128), 1)
         at = d * 64
-        t_ref[at : at + 64, 0:128] = rows(flat, d * 64, 64, 192)
-        t_ref[at : at + 64, 128:256] = rows(flat, d * 64 + jnp.maximum(sx - 1, 0), 64, 192)
+        t_ref[at : at + 64, 0:128] = block[d, 0]
+        t_ref[at : at + 64, 128:256] = block[d, jnp.maximum(sx - 1, 0)]
         t_ref[at : at + 64, 256:384] = jnp.where(lane < 64, low, high)
 
 
@@ -107,13 +106,13 @@
         yw[k + 128 : k + 256, 128:] = zero
 
 
-def zy_chunk(k, own2, other2, zl, yw, tb, out):
+def zy_chunk(k, own, other, zl, yw, tb, out):
     for pair in range(12):
         tops, lows = [], []
         for n in (2 * pair, 2 * pair + 1):
-            start = n // 8 * 64 + n % 8 + k * 8
+            at = (n // 8, n % 8 + k * 8)
             top, low = split(
-                jnp.concatenate([rows(own2, start, 64, 192), rows(other2, start, 64, 192)], axis=0)
+                jnp.concatenate([own[at], other[at]], axis=0)
             )
             tops.append(top)
             lows.append(low)
@@ -150,7 +149,7 @@
     me = z * 4 + x
 
     def dev(a, yy):
-        return (a // 4 * 16 + yy * 4 + a % 4, s)
+        return ((a >> 2) * 16 + yy * 4 + (a & 3), s)
 
     partner = (p, 1 - s)
 
@@ -163,7 +162,7 @@
 
     def greet(d, c):
         pl.semaphore_signal(
-            barrier, inc=1, device_id=dev((me + d) % 32, y), device_id_type=MESH
+            barrier, inc=1, device_id=dev((me + d) & 31, y), device_id_type=MESH
         )
         return c
 
@@ -178,105 +177,123 @@
 
     lax.fori_loop(1, 4, greet_y, 0)
 
-    load = pltpu.make_async_copy(field.at[0], block, lsem.at[0])
-    load.start()
     smalls = [
         pltpu.make_async_copy(a.at[0], b, wsem.at[n])
         for n, (a, b) in enumerate(
-            ((zm, zm_ref), (ym, ym_ref), (mz, mz_ref), (mx, mx_ref), (my, my_ref))
+            ((mz, mz_ref), (mx, mx_ref), (my, my_ref), (zm, zm_ref), (ym, ym_ref))
         )
     ]
     for c in smalls:
         c.start()
-    for c in smalls:
+    for d in range(3):
+
+        def load_row(x, c):
+            pltpu.make_async_copy(
+                field.at[0, :, d, x, 0], block.at[d, x], lsem.at[d]
+            ).start()
+            return c
+
+        lax.fori_loop(0, 64, load_row, 0, unroll=4)
+    for c in smalls[:3]:
         c.wait()
     face_rows(sizes_ref, mx_ref, my_ref, e_ref)
-    zy_weights(sizes_ref, s, zm_ref, ym_ref, zl, yw)
     lane1 = lax.broadcasted_iota(jnp.int32, (1, 128), 1)
     row = jnp.where(lane1 == 0, match_ref[0, 0], match_ref[0, 1])
     row = jnp.where(lane1 == 2, match_ref[0, 2], row)
-    mt[me] = jnp.where(lane1 == 3, match_ref[0, 3], row)
-    load.wait()
+    row = jnp.where(lane1 == 3, match_ref[0, 3], row)
+    q = row >> 2
+    mt[me] = ((((q >> 2) & 3) * 32 + (q >> 4) * 4 + (q & 3)) << 2) + (row & 3)
+    for d in range(3):
+        pltpu.make_async_copy(block.at[d], block.at[d], lsem.at[d]).wait()
     trace_part(sizes_ref, block, t_ref)
+    parts = mortar_part(t_ref, s, mz_ref, e_ref)
+    half = s == 0
+    for d in range(3):
+        part[d] = jnp.where(half, parts[d][:, 128:], parts[d][:, :128])
+    for d in range(3):
+        mine[:, d, :] = jnp.where(half, parts[d][:, :128], parts[d][:, 128:])
+    mine[:, 3, :] = jnp.zeros((32, 128), F32)
     pl.semaphore_wait(barrier, 35)
-
-    def field_copy(k):
-        at = pl.ds(pl.multiple_of(k * 8, 8), 8)
-        return copy(field.at[0, :, :, at], other.at[:, :, at], fsem, k, partner)
-
-    def start_field(k, c):
-        field_copy(k).start()
-        return c
-
-    lax.fori_loop(0, 8, start_field, 0)
+    c0 = copy(part, got, psem, 0, partner)
+    c0.start()
+
+    def field_start(k, c):
+        for d in range(3):
+            for n in range(8):
+                x = k * 8 + n
+                copy(field.at[0, :, d, x, 0], other.at[d, x], fsem, k, partner).start()
+        return c
+
+    def field_wait(k):
+        at = other.at[:, pl.ds(pl.multiple_of(k * 8, 8), 8)]
+        copy(at, at, fsem, k, partner).wait()
 
     def match_copy(d):
-        return copy(mt.at[me], mt.at[me], asem, d, dev((me + d) % 32, y))
+        return copy(mt.at[me], mt.at[me], asem, d, dev((me + d) & 31, y))
 
     def start_match(d, c):
         match_copy(d).start()
         return c
 
     lax.fori_loop(1, 32, start_match, 0)
-
-    parts = mortar_part(t_ref, s, mz_ref, e_ref)
-    half = s == 0
-    for d in range(3):
-        part[d] = jnp.where(half, parts[d][:, 128:], parts[d][:, :128])
-    c0 = copy(part, got, psem, 0, partner)
-    c0.start()
-    for d in range(3):
-        mine[:, d, :] = jnp.where(half, parts[d][:, :128], parts[d][:, 128:])
-    mine[:, 3, :] = jnp.zeros((32, 128), F32)
-
-    own2 = block.reshape(64 * 192, 128)
-    other2 = other.reshape(64 * 192, 128)
-
-    def mid_copy(k):
-        at = pl.ds(pl.multiple_of(k * 8, 8), 8)
-        return pltpu.make_async_copy(stage.at[k % 2], mid.at[:, :, at], osem.at[k % 2])
+    field_start(0, 0)
+
+
+    def mid_start(k):
+        for m in range(2):
+            for d in range(3):
+                for n in range(8):
+                    pltpu.make_async_copy(
+                        stage.at[k % 2, m, d, n], mid.at[m, d, :, k * 8 + n, 0], osem.at[k % 2]
+                    ).start()
+
+    def mid_wait(k):
+        pltpu.make_async_copy(stage.at[k % 2], stage.at[k % 2], osem.at[k % 2]).wait()
 
     def chunks(lo, hi):
         def one(k, c):
-            field_copy(k).wait()
+            field_wait(k)
 
             @pl.when(k >= 2)
             def _():
-                mid_copy(k - 2).wait()
-
-            zy_chunk(k, own2, other2, zl, yw, tb, stage.at[k % 2])
-            mid_copy(k).start()
+                mid_wait(k - 2)
+
+            zy_chunk(k, block, other, zl, yw, tb, stage.at[k % 2])
+            mid_start(k)
             return c
 
         lax.fori_loop(lo, hi, one, 0)
 
-    chunks(0, CUTS[0])
     c0.wait()
     for d in range(3):
         mine[:, d, :] = mine[:, d, :] + got[d]
 
     def spread_copy(d):
-        a = (me + d) % 32
-        return copy(mine.at[a], gath.at[y, me], bsem, d, dev(a, y))
+        a = (me + d) & 31
+        return copy(mine.at[a], gath.at[y * 32 + me], bsem, d, dev(a, y))
 
     def start_spread(d, c):
         spread_copy(d).start()
         return c
 
     lax.fori_loop(1, 32, start_spread, 0)
+    lax.fori_loop(1, 8, field_start, 0)
     cm = copy(mine, own_ref.at[s], psem, 1, partner)
     cm.start()
     own_ref[s] = mine[...]
-    gath[y, me] = mine[me]
+    gath[y * 32 + me] = mine[me]
 
     def wait_match(d, c):
         match_copy(d).wait()
         return c
 
     lax.fori_loop(1, 32, wait_match, 0)
-    tos = pltpu.make_async_copy(mt, mts, lsem.at[1])
+    tos = pltpu.make_async_copy(mt, mts, lsem.at[3])
     tos.start()
-    chunks(CUTS[0], CUTS[1])
+    for c in smalls[3:]:
+        c.wait()
+    zy_weights(sizes_ref, s, zm_ref, ym_ref, zl, yw)
+    chunks(0, CUTS[1])
 
     def wait_spread(d, c):
         spread_copy(d).wait()
@@ -285,7 +302,8 @@
     lax.fori_loop(1, 32, wait_spread, 0)
 
     def line_copy(d):
-        return copy(gath.at[y], gath.at[y], csem, d, dev(me, (y + d) % 4))
+        at = gath.at[pl.ds(pl.multiple_of(y * 32, 32), 32)]
+        return copy(at, at, csem, d, dev(me, (y + d) % 4))
 
     for d in range(1, 4):
         line_copy(d).start()
@@ -296,27 +314,26 @@
 
     lane4 = lax.broadcasted_iota(jnp.int32, (4, 128), 1) // 32
 
-    def pick(a, c):
+    def pick(d, c):
+        a = (me + d) & 31
         out = jnp.zeros((4, 128), F32)
         for f in range(4):
             m = mts[a, 0, f]
-            q = m // 4
-            v = gath[q // 4 % 4, q // 16 * 4 + q % 4]
-            v = pltpu.roll(v, (f + 4 - m % 4) % 4 * 32, 1)
+            v = pltpu.roll(gath[m >> 2], ((f - m) & 3) * 32, 1)
             out = jnp.where(lane4 == f, v, out)
         sendb[a] = out
         return c
 
-    lax.fori_loop(0, 32, pick, 0, unroll=4)
-
     def back_copy(d):
-        a = (me + d) % 32
+        a = (me + d) & 31
         return copy(sendb.at[a], near_ref.at[s, me], dsem, d, dev(a, y))
 
     def start_back(d, c):
         back_copy(d).start()
         return c
 
+    lax.fori_loop(1, 17, pick, 0, unroll=8)
+    lax.fori_loop(17, 33, pick, 0, unroll=8)
     lax.fori_loop(1, 32, start_back, 0)
     near_ref[s, me] = sendb[me]
     chunks(CUTS[2], 8)
@@ -329,12 +346,12 @@
     cn = copy(near_ref.at[s], near_ref.at[s], psem, 2, partner)
     cn.start()
     cm.wait()
-    mid_copy(6).wait()
-    mid_copy(7).wait()
+    mid_wait(6)
+    mid_wait(7)
     cn.wait()
 
 
-CUTS = (1, 4, 6)
+CUTS = (0, 3, 6)
 
 
 def front(sizes, matching, field, zm, ym, mz, mx, my):
@@ -345,12 +362,12 @@
     shape = jax.ShapeDtypeStruct((2, 32, 4, 128), F32)
     return pl.pallas_call(
         front_kernel,
-        out_shape=(shape, shape, jax.ShapeDtypeStruct((2, 3, 64, 64, 128), F32)),
+        out_shape=(shape, shape, jax.ShapeDtypeStruct((2, 3, 64, 64, 1, 128), F32)),
         in_specs=[smem, smem] + [hbm] * 6,
         out_specs=(vmem, vmem, hbm),
         scratch_shapes=[
-            pltpu.VMEM((64, 3, 64, 128), F32),
-            pltpu.VMEM((64, 3, 64, 128), F32),
+            pltpu.VMEM((3, 64, 64, 128), F32),
+            pltpu.VMEM((3, 64, 64, 128), F32),
             pltpu.VMEM((2, 128, 128), F32),
             pltpu.VMEM((2, 128, 128), F32),
             pltpu.VMEM((4, 32, 128), F32),
@@ -365,11 +382,11 @@
             pltpu.VMEM((3, 32, 128), F32),
             pltpu.VMEM((3, 32, 128), F32),
             pltpu.VMEM((32, 4, 128), F32),
-            pltpu.VMEM((4, 32, 4, 128), F32),
+            pltpu.VMEM((128, 4, 128), F32),
             pltpu.VMEM((32, 4, 128), F32),
             pltpu.VMEM((32, 1, 128), jnp.int32),
             pltpu.SMEM((32, 1, 128), jnp.int32),
-            dma((2,)), dma((5,)), dma((2,)), dma((2, 8)), dma((2, 3)),
+            dma((4,)), dma((5,)), dma((2,)), dma((2, 8)), dma((2, 3)),
             dma((2, 32)), dma((2, 32)), dma((2, 4)), dma((2, 32)),
         ],
         compiler_params=pltpu.CompilerParams(
@@ -429,7 +446,7 @@
 
 def last_kernel(
     sizes_ref, cpl, orient_ref, data, xm_ref, own_ref, near_ref, mz_ref, mx_ref, my_ref, out,
-    xl, e_ref, bx, by,
+    xl, cs, e_ref, bx, by,
 ):
     i = pl.program_id(0)
     sx, sy = sizes_ref[0, 0], sizes_ref[0, 1]
@@ -446,6 +463,11 @@
         xl[:64, 128:] = hi
         xl[64:, :128] = jnp.concatenate([l0, l1], axis=1)
         xl[64:, 128:] = jnp.zeros((64, 128), BF16)
+        for c in range(3):
+            for d in range(3):
+                cs[c * 3 + d : c * 3 + d + 1, :] = jnp.broadcast_to(
+                    cpl[c : c + 1, d : d + 1], (1, 256)
+                )
         face_rows(sizes_ref, mx_ref, my_ref, e_ref)
         back_part(orient_ref, own_ref, near_ref, mz_ref, e_ref, lax.axis_index("slab"), bx, by)
 
@@ -455,7 +477,6 @@
     last_x = row == sx - 1
     first_y = lane == 0
     last_y = lane == sy - 1
-    flat = data.reshape(2 * 3 * 64 * 8, 128)
     cols = [pltpu.roll(by[c], lax.rem(128 - i * 8, 128), 1) for c in range(3)]
     for pair in range(4):
         inner = []
@@ -463,9 +484,7 @@
             tops, lows = [], []
             for n in range(2):
                 k = pair * 2 + n
-                first = rows(flat, d * 512 + k, 64, 8)
-                second = rows(flat, 1536 + d * 512 + k, 64, 8)
-                top, low = split(jnp.concatenate([first, second], axis=0))
+                top, low = split(jnp.concatenate([data[0, d, k], data[1, d, k]], axis=0))
                 tops.append(top)
                 lows.append(low)
             w = jnp.concatenate(
@@ -474,7 +493,9 @@
             r = bdot(xl[...], w)
             inner.append(r[:64] + r[64:])
         for c in range(3):
-            mix = cpl[0, c, 0] * inner[0] + cpl[0, c, 1] * inner[1] + cpl[0, c, 2] * inner[2]
+            at = c * 3
+            mix = cs[at : at + 1, :] * inner[0] + cs[at + 1 : at + 2, :] * inner[1]
+            mix = mix + cs[at + 2 : at + 3, :] * inner[2]
             for n in range(2):
                 k = pair * 2 + n
                 v = mix[:, n * 128 : n * 128 + 128]
@@ -495,9 +516,9 @@
         out_shape=jax.ShapeDtypeStruct((1, 64, 3, 64, 128), F32),
         in_specs=[
             smem,
+            whole(None, 3, 3),
             smem,
-            smem,
-            pl.BlockSpec((2, 3, 64, 8, 128), lambda i: (0, 0, 0, i, 0)),
+            pl.BlockSpec((2, 3, 8, 64, 128), lambda i: (0, 0, i, 0, 0)),
             whole(None, 2, 64, 64),
             whole(2, 32, 4, 128),
             whole(2, 32, 4, 128),
@@ -508,6 +529,7 @@
         out_specs=pl.BlockSpec((None, 8, 3, 64, 128), lambda i: (0, i, 0, 0, 0)),
         scratch_shapes=[
             pltpu.VMEM((128, 256), BF16),
+            pltpu.VMEM((16, 256), F32),
             pltpu.VMEM((256, 384), F32),
             pltpu.VMEM((2, 3, 64, 128), F32),
             pltpu.VMEM((3, 128, 128), F32),
@@ -520,9 +542,10 @@
 def per_device(
     field, xmats, ymats, zmats, coupling, mortar_z, mortar_x, mortar_y, matching, orient, sizes
 ):
+    field = field.reshape(1, 64, 3, 64, 1, 128)
     own, near, mid = front(sizes, matching, field, zmats, ymats, mortar_z, mortar_x, mortar_y)
     return first_spread(
-        sizes, coupling, orient, mid, xmats, own, near, mortar_z, mortar_x, mortar_y
+        sizes, coupling, orient, mid.reshape(2, 3, 64, 64, 128), xmats, own, near, mortar_z, mortar_x, mortar_y
     )
 
 

time: 69.5 us -> 55.6 us (0.80)
  Pallas kernels: 68 us -> 54.1 us
    pallas_call x1, Pallas kernels: 54.6 us -> 41.4 us  [front(): pl.pallas_call(front_kernel, out_shape=(shape, shape, jax.ShapeDtypeStruc...]
    pallas_call x1, Pallas kernels: 13.4 us -> 12.7 us  [first_spread(): pl.pallas_call(last_kernel, grid=(8,), out_shape=jax.ShapeDtypeStruct((1,...]
where the time goes in v1:
time: 55.6 us; the launch traced here: 55.4 us
  Pallas kernels  54.1 us (97%)
  local copies, waits for them, and re-layouts  1.27 us (2%)
    pallas_call x1, Pallas kernels, front(): pl.pallas_call(front_kernel, out_shape=(shape, shape, jax.ShapeDtypeStruc...  41.4 us
    pallas_call x1, Pallas kernels, first_spread(): pl.pallas_call(last_kernel, grid=(8,), out_shape=jax.ShapeDtypeStruct((1,...  12.7 us
    unnamed x1, local copies, waits for them, and re-layouts  1.27 us

profile of v1, /device:TPU:1, one launch (start us, length us, event | category | flops | bytes accessed | tf_op | source)
XLA Modules:
  0.0 55.4 jit_solution(10350781938505861700)
XLA Ops:
  0.0 1.3 %copy.12.cpl = f32[1,3,3]{2,1,0:T(4,128)} copy(f32[1,3,3]{2,0,1:T(1,128)} %param.15) | data formatting | bytes 72 | tf_op args[4]
  1.3 41.4 %front.1 = (f32[2,32,4,128]{3,2,1,0:T(4,128)}, f32[2,32,4,128]{3,2,1,0:T(4,128)}, f32[2,3,64,64,1,128]{5,4,3,2,1,0:T(1,128)}) custom-call(s32[1,2]{1,0:T(1,128)} %sizes_ref.3, s32[1,4]{1,0:T(1,128)} %match_ref.1, f32[1,64,3,64,1,128]{5,4,3,2,1,0:T(1,128)} %bitcast.3, f32[1,2,128,128]{3,2,1,0:T(8,128)} %zm.1, f32[1,2,128,128]{3,2,1,0:T(8,128)} %ym.1, ...), custom_call_target="tpu_custom_call" | custom-call | tf_op jit(solution)/shard_map/front/pallas_call | solution.py:363
  42.7 12.7 %first_spread.1 = f32[1,64,3,64,128]{4,3,2,1,0:T(8,128)} custom-call(s32[1,2]{1,0:T(1,128)} %sizes_ref.3, f32[1,3,3]{2,1,0:T(4,128)} %copy.12.cpl, s32[1,4]{1,0:T(1,128)} %orient_ref.1, f32[2,3,64,64,128]{4,3,2,1,0:T(8,128)} %bitcast.2, f32[1,2,64,64]{3,2,1,0:T(8,128)} %xm_ref.1, f32[2,32,4,128]{3,2,1,0:T(4,128)} %get-tuple-element.9.own_ref, ...), custom_call_target="tpu_custom_call" | custom-call | tf_op jit(solution)/shard_map/first_spread/pallas_call | solution.py:513

commit v2 on v1

--- a/solution.py
+++ b/solution.py
@@ -466,15 +466,13 @@
         for c in range(3):
             for d in range(3):
                 cs[c * 3 + d : c * 3 + d + 1, :] = jnp.broadcast_to(
-                    cpl[c : c + 1, d : d + 1], (1, 256)
+                    cpl[c, :, d : d + 1], (1, 256)
                 )
         face_rows(sizes_ref, mx_ref, my_ref, e_ref)
         back_part(orient_ref, own_ref, near_ref, mz_ref, e_ref, lax.axis_index("slab"), bx, by)
 
-    row = lax.broadcasted_iota(jnp.int32, (64, 128), 0)
     lane = lax.broadcasted_iota(jnp.int32, (64, 128), 1)
-    first_x = row == 0
-    last_x = row == sx - 1
+    last_x = pl.ds(jnp.maximum(sx - 1, 0), 1)
     first_y = lane == 0
     last_y = lane == sy - 1
     cols = [pltpu.roll(by[c], lax.rem(128 - i * 8, 128), 1) for c in range(3)]
@@ -500,11 +498,10 @@
                 k = pair * 2 + n
                 v = mix[:, n * 128 : n * 128 + 128]
                 zrow = pl.ds(i * 8 + k, 1)
-                v = v + jnp.where(first_x, bx[0, c, zrow, :], 0.0)
-                v = v + jnp.where(last_x, bx[1, c, zrow, :], 0.0)
-                v = v + jnp.where(first_y, cols[c][:64, k : k + 1], 0.0)
-                v = v + jnp.where(last_y, cols[c][64:, k : k + 1], 0.0)
-                out[k, c] = v
+                edge = jnp.where(last_y, cols[c][64:, k : k + 1], 0.0)
+                out[k, c] = v + jnp.where(first_y, cols[c][:64, k : k + 1], edge)
+                out[k, c, :1, :] = out[k, c, :1, :] + bx[0, c, zrow, :]
+                out[k, c, last_x, :] = out[k, c, last_x, :] + bx[1, c, zrow, :]
 
 
 def first_spread(sizes, cpl, orient, data, xm, own, near, mz, mx, my):
@@ -516,7 +513,7 @@
         out_shape=jax.ShapeDtypeStruct((1, 64, 3, 64, 128), F32),
         in_specs=[
             smem,
-            whole(None, 3, 3),
+            whole(3, 1, 3),
             smem,
             pl.BlockSpec((2, 3, 8, 64, 128), lambda i: (0, 0, i, 0, 0)),
             whole(None, 2, 64, 64),
@@ -545,7 +542,7 @@
     field = field.reshape(1, 64, 3, 64, 1, 128)
     own, near, mid = front(sizes, matching, field, zmats, ymats, mortar_z, mortar_x, mortar_y)
     return first_spread(
-        sizes, coupling, orient, mid.reshape(2, 3, 64, 64, 128), xmats, own, near, mortar_z, mortar_x, mortar_y
+        sizes, coupling.transpose(1, 0, 2), orient, mid.reshape(2, 3, 64, 64, 128), xmats, own, near, mortar_z, mortar_x, mortar_y
     )
 
 

time: 55.6 us -> 54.6 us (0.982)
  local copies, waits for them, and re-layouts: 1.27 us -> 0 us
    unnamed x1 -> x0, local copies, waits for them, and re-layouts: 1.27 us -> none
where the time goes in v2:
time: 54.6 us; the launch traced here: 54.4 us
  Pallas kernels  54.4 us (100%)
    pallas_call x1, Pallas kernels, front(): pl.pallas_call(front_kernel, out_shape=(shape, shape, jax.ShapeDtypeStruc...  41.5 us
    pallas_call x1, Pallas kernels, first_spread(): pl.pallas_call(last_kernel, grid=(8,), out_shape=jax.ShapeDtypeStruct((1,...  12.9 us

profile of v2, /device:TPU:1, one launch (start us, length us, event | category | flops | bytes accessed | tf_op | source)
XLA Modules:
  0.0 54.4 jit_solution(5540140657824120602)
XLA Ops:
  0.0 41.5 %front.1 = (f32[2,32,4,128]{3,2,1,0:T(4,128)}, f32[2,32,4,128]{3,2,1,0:T(4,128)}, f32[2,3,64,64,1,128]{5,4,3,2,1,0:T(1,128)}) custom-call(s32[1,2]{1,0:T(1,128)} %sizes_ref.3, s32[1,4]{1,0:T(1,128)} %match_ref.1, f32[1,64,3,64,1,128]{5,4,3,2,1,0:T(1,128)} %bitcast.4, f32[1,2,128,128]{3,2,1,0:T(8,128)} %zm.1, f32[1,2,128,128]{3,2,1,0:T(8,128)} %ym.1, ...), custom_call_target="tpu_custom_call" | custom-call | tf_op jit(solution)/shard_map/front/pallas_call | solution.py:363
  41.5 12.9 %first_spread.1 = f32[1,64,3,64,128]{4,3,2,1,0:T(8,128)} custom-call(s32[1,2]{1,0:T(1,128)} %sizes_ref.3, f32[3,1,3]{2,1,0:T(1,128)} %bitcast.5, s32[1,4]{1,0:T(1,128)} %orient_ref.1, f32[2,3,64,64,128]{4,3,2,1,0:T(8,128)} %bitcast.3, f32[1,2,64,64]{3,2,1,0:T(8,128)} %xm_ref.1, f32[2,32,4,128]{3,2,1,0:T(4,128)} %get-tuple-element.9.own_ref, ...), custom_call_target="tpu_custom_call" | custom-call | tf_op jit(solution)/shard_map/first_spread/pallas_call | solution.py:510
